TPU v7x, 32 devices: a whole 2x2x4 slice. The times are simulated.
32 devices in a mesh: frow: 4 (over y, x), fcol: 8 (over z, core).
Axes of the slice: x: 2, y: 2, z: 4, core: 2. Of those that a mesh axis runs over, the one named last changes fastest.
Arguments:
- strips: bfloat16 [2, 256, 32768], P(None, 'frow', 'fcol'), may hold values from -6 to 6
- row_window: float32 [4096], replicated, may hold values from 0.5 to 2
- col_window: float32 [4096], replicated, may hold values from 0.5 to 2
- sub_rows: int32 [4], replicated, may hold values from 0 to 65535
- sub_cols: int32 [4], replicated, may hold values from 0 to 65535
- facet_offsets: int32 [4, 8, 2], replicated, may hold values from 0 to 65472, as said below
- owner_map: int32 [32], replicated, may hold values from 0 to 31, each once
- screens: float32 [2, 32, 512, 256], P(None, 'fcol', 'frow'), may hold values from -1.5 to 1.5
Outputs:
- subgrids: float32 [2, 32, 512, 256], P(None, 'fcol', 'frow')
Inputs may be any that keep to these rules, and one draw needn't show every extreme that they name: `facet_offsets`: entry [a, b, 0] is a multiple of 64 whose 64 rows stay within one facet of 4096 rows; entry [a, b, 1] is a multiple of 4096.
All inputs are finite; a program needn't handle non-finite values.
Results may differ from a plain program's by a relative error of at most 0.0066.
Values may be sent and summed in bfloat16 or wider, within the bound.
A program may use at most 128 MiB of HBM per device.

v0:
```python
import math

import jax
import jax.numpy as jnp
import ml_dtypes
import numpy as np
from jax import lax
from jax.sharding import PartitionSpec as P

N = 65536
F = 4096
R = 64
M = 128
S = 512
SG_R = 4
SG_C = 4
PIECES = 32
CHUNK = 32


def mod_product(first_factor, second_factor):
    upper_part = first_factor // 256
    lower_part = first_factor % 256
    return (((upper_part * second_factor) & (N - 1)) * 256 + lower_part * second_factor) & (N - 1)


def turn(phase, period):
    angle = phase.astype(jnp.float32) * (2.0 * math.pi / period)
    return jnp.cos(angle), jnp.sin(angle)


def dft_constant():
    phase = (np.arange(F)[:, None] * np.arange(M)[None, :] % N) * (2.0 * math.pi / N)
    return np.concatenate([np.cos(phase), -np.sin(phase)], 1).astype(ml_dtypes.bfloat16)


def expansion_constant():
    phase = (np.arange(M)[:, None] * np.arange(S // 2)[None, :] % S) * (2.0 * math.pi / S)
    return np.cos(phase).astype(np.float32), np.sin(phase).astype(np.float32)


def partials(strips, first_col, col_window, sub_cols):
    positions = first_col + jnp.arange(F, dtype=jnp.int32)
    cos, sin = turn(mod_product(positions[None, :], sub_cols[:, None]), N)
    real = (col_window[None, :] * cos)[:, None]
    imag = (-col_window[None, :] * sin)[:, None]
    strip_real = strips[0].astype(jnp.float32)[None]
    strip_imag = strips[1].astype(jnp.float32)[None]
    turned = jnp.stack(
        [strip_real * real - strip_imag * imag, strip_real * imag + strip_imag * real], 1
    ).astype(jnp.bfloat16)
    product = jnp.dot(
        turned.reshape(SG_C * 2 * R, F), jnp.asarray(dft_constant()), preferred_element_type=jnp.float32
    ).reshape(SG_C, 2, R, 2, M)
    part_real = product[:, 0, :, 0] - product[:, 1, :, 1]
    part_imag = product[:, 0, :, 1] + product[:, 1, :, 0]
    band = first_col // (N // S)
    cos, sin = turn((band * jnp.arange(M, dtype=jnp.int32)) & (S - 1), S)
    return jnp.concatenate(
        [part_real * cos + part_imag * sin, part_imag * cos - part_real * sin], -1
    ).astype(jnp.bfloat16)


def expansion(band):
    base_real, base_imag = expansion_constant()
    cos, sin = turn((band[:, None] * jnp.arange(S // 2, dtype=jnp.int32)) & (S - 1), S)
    real = base_real[None] * cos[:, None] - base_imag[None] * sin[:, None]
    imag = base_real[None] * sin[:, None] + base_imag[None] * cos[:, None]
    return jnp.concatenate(
        [jnp.concatenate([real, imag], -1), jnp.concatenate([-imag, real], -1)], 1
    ).astype(jnp.bfloat16)


def placed_rows(first_row, row_start, rows, row_window, slot_rows):
    inner = jnp.arange(R, dtype=jnp.int32)
    window = jax.vmap(lambda start: lax.dynamic_slice_in_dim(row_window, start, R))(first_row % F)
    position = (first_row[:, None] + inner[None]).reshape(1, -1)
    shift = (row_start - first_row // (N // S)) & (S - 1)
    shift = jnp.where(shift < M, shift, shift - S)
    row_ids = jnp.arange(rows, dtype=jnp.int32)[:, None]
    row_index = row_ids + jnp.repeat(shift, R)[None]
    scale = jnp.where((row_index >= 0) & (row_index < M), window.reshape(1, -1), 0.0)
    base_cos, base_sin = turn((row_ids * position) & (N - 1), N)
    base_cos = base_cos * scale
    base_sin = base_sin * scale
    frequency = (slot_rows[:, None] + jnp.repeat(shift, R)[None]) & (N - 1)
    cos, sin = turn(mod_product(position, frequency), N)
    real = base_cos[None] * cos[:, None] - base_sin[None] * sin[:, None]
    imag = -(base_cos[None] * sin[:, None] + base_sin[None] * cos[:, None])
    return jnp.stack([real, imag], 1).astype(jnp.bfloat16)


def shards(strips, row_window, col_window, sub_rows, sub_cols, facet_offsets, owner_map, screens):
    row_index = lax.axis_index("frow")
    col_index = lax.axis_index("fcol")
    col_count = lax.axis_size("fcol")
    row_devices = lax.axis_size("frow")
    slot_count = PIECES // col_count
    rows = S // row_devices
    sources = row_devices * col_count
    own = partials(strips, facet_offsets[row_index, col_index, 1], col_window, sub_cols)
    slots = lax.dynamic_slice_in_dim(owner_map, col_index * slot_count, slot_count)
    if slot_count < SG_C:
        outgoing = jnp.take(own, owner_map // 2 % SG_C, axis=0)
        picked = lax.all_to_all(outgoing, "fcol", split_axis=0, concat_axis=0, tiled=True)
        picked = picked.reshape(col_count, slot_count, R, 2 * M)
        picked = lax.all_gather(picked, "frow", tiled=True)
    else:
        picked = lax.all_gather(own, ("frow", "fcol"))
        picked = jnp.take(picked, slots // 2 % SG_C, axis=1)
    lanes = jnp.arange(2 * M, dtype=jnp.int32)
    signs = (1 - 2 * ((lanes[None] * (slots % 2)[:, None]) & 1)).astype(jnp.bfloat16)
    picked = picked * signs[None, :, None, :]
    first = facet_offsets.reshape(sources, 2)
    slot_rows = sub_rows[slots // (2 * SG_C)]

    def gather_part(first, picked):
        count = first.shape[0]
        row_part = placed_rows(first[:, 0], row_index * rows, rows, row_window, slot_rows)
        table = expansion(first[:, 1] // (N // S))
        spread = jnp.einsum("nsxk,nkv->snxv", picked, table, preferred_element_type=jnp.float32)
        spread = spread.astype(jnp.bfloat16).reshape(slot_count, count * R, S)
        return jnp.einsum(
            "spkc,scv->spkv", row_part, spread, preferred_element_type=jnp.float32
        )

    chunk = min(CHUNK, sources)
    if sources == chunk:
        total = gather_part(first, picked)
    else:
        steps = sources // chunk
        total, unused = lax.scan(
            lambda carry, item: (carry + gather_part(*item), None),
            jnp.zeros((slot_count, 2, rows, S), jnp.float32),
            (first.reshape(steps, chunk, 2), picked.reshape(steps, chunk, slot_count, R, 2 * M)),
        )
    half = S // 2
    weight = 2.0 / math.sqrt(sources) / math.sqrt(M) / math.sqrt(R * F)
    grid_real = (total[:, 0, :, :half] - total[:, 1, :, half:]) * weight
    grid_imag = (total[:, 0, :, half:] + total[:, 1, :, :half]) * weight
    return jnp.stack(
        [
            screens[0] * grid_real - screens[1] * grid_imag,
            screens[0] * grid_imag + screens[1] * grid_real,
        ],
        0,
    )


def solution(mesh):
    return jax.shard_map(
        shards,
        mesh=mesh,
        in_specs=(
            P(None, "frow", "fcol"),
            P(),
            P(),
            P(),
            P(),
            P(),
            P(),
            P(None, "fcol", "frow", None),
        ),
        out_specs=P(None, "fcol", "frow", None),
        check_vma=False,
    )
```

profile of v0, /device:TPU:0, one launch (start us, length us, event | category | flops | bytes accessed | tf_op | source)
XLA Modules:
  0.0 131.1 jit_solution(12431433495608172296)
XLA Ops:
  6.5 1.3 constant_dynamic-slice_fusion.1
  10.4 0.7 neg.19
  11.1 1.4 %bitcast_convert_fusion.1 = (f32[64,4096]{1,0:T(8,128)S(1)}, f32[64,4096]{1,0:T(8,128)S(1)}) fusion(bf16[2,64,4096]{2,1,0:T(8,128)(2,1)} %param.13), kind=kLoop, calls=%fused_computation.46 | loop fusion | flops 524288 | bytes 3145728 | tf_op jit(solution)/shard_map/mul | solution.py:50
  13.3 1.5 %cosine_multiply_fusion = (f32[4,4096]{1,0:T(4,128)S(1)}, f32[4,4096]{1,0:T(4,128)S(1)}) fusion(s32[4096]{0:T(1024)S(1)} %get-tuple-element.52, s32[4]{0:T(128)} %param.17, s32[4096]{0:T(1024)S(1)} %get-tuple-element.53, f32[4096]{0:T(1024)} %param.15, f32[4096]{0:T(1024)S(1)} %neg.19), kind=kLoop, calls=%fused_computation.61 | loop fusion | flops 163840 | bytes 196624 | tf_op jit(solution)/shard_map/mul | solution.py:45
  14.7 1.0 subtract_convert_fusion
  15.8 1.3 fusion.13
  17.2 0.7 pad_maximum_fusion.1
  18.4 65.3 %while.1 = (s32[]{:T(128)}, f32[4096]{0:T(1024)}, s32[32,1]{0,1:T(1,128)S(1)}, f32[32,64]{1,0:T(8,128)S(1)}, s32[]{:T(128)}, /*index=5*/s32[]{:T(128)}) while((s32[]{:T(128)}, f32[4096]{0:T(1024)}, s32[32,1]{0,1:T(1,128)S(1)}, f32[32,64]{1,0:T(8,128)S(1)}, s32[]{:T(128)}, /*index=5*/s32[]{:T(128)}) %tuple.35), condition=%wide.while_cond, body=%wide.while_body.sunk | while | flops 2 | bytes 1113 | solution.py:76
  19.1 1.4 %dynamic-slice_bitcast_fusion.2 = f32[1,64]{1,0:T(1,128)S(1)} fusion(f32[4096]{0:T(1024)} %get-tuple-element.94, s32[]{:T(128)} %bitcast.121), kind=kLoop, calls=%fused_computation.2.clone.1 | loop fusion | bytes 516 | tf_op jit(solution)/shard_map/vmap()/gather
  21.1 1.4 %dynamic-slice_bitcast_fusion.2 = f32[1,64]{1,0:T(1,128)S(1)} fusion(f32[4096]{0:T(1024)} %get-tuple-element.94, s32[]{:T(128)} %bitcast.121), kind=kLoop, calls=%fused_computation.2.clone.1 | loop fusion | bytes 516 | tf_op jit(solution)/shard_map/vmap()/gather
  23.1 1.4 %dynamic-slice_bitcast_fusion.2 = f32[1,64]{1,0:T(1,128)S(1)} fusion(f32[4096]{0:T(1024)} %get-tuple-element.94, s32[]{:T(128)} %bitcast.121), kind=kLoop, calls=%fused_computation.2.clone.1 | loop fusion | bytes 516 | tf_op jit(solution)/shard_map/vmap()/gather
  25.2 1.4 %dynamic-slice_bitcast_fusion.2 = f32[1,64]{1,0:T(1,128)S(1)} fusion(f32[4096]{0:T(1024)} %get-tuple-element.94, s32[]{:T(128)} %bitcast.121), kind=kLoop, calls=%fused_computation.2.clone.1 | loop fusion | bytes 516 | tf_op jit(solution)/shard_map/vmap()/gather
  27.2 1.4 %dynamic-slice_bitcast_fusion.2 = f32[1,64]{1,0:T(1,128)S(1)} fusion(f32[4096]{0:T(1024)} %get-tuple-element.94, s32[]{:T(128)} %bitcast.121), kind=kLoop, calls=%fused_computation.2.clone.1 | loop fusion | bytes 516 | tf_op jit(solution)/shard_map/vmap()/gather
  29.2 1.4 %dynamic-slice_bitcast_fusion.2 = f32[1,64]{1,0:T(1,128)S(1)} fusion(f32[4096]{0:T(1024)} %get-tuple-element.94, s32[]{:T(128)} %bitcast.121), kind=kLoop, calls=%fused_computation.2.clone.1 | loop fusion | bytes 516 | tf_op jit(solution)/shard_map/vmap()/gather
  31.3 1.4 %dynamic-slice_bitcast_fusion.2 = f32[1,64]{1,0:T(1,128)S(1)} fusion(f32[4096]{0:T(1024)} %get-tuple-element.94, s32[]{:T(128)} %bitcast.121), kind=kLoop, calls=%fused_computation.2.clone.1 | loop fusion | bytes 516 | tf_op jit(solution)/shard_map/vmap()/gather
  33.3 1.4 %dynamic-slice_bitcast_fusion.2 = f32[1,64]{1,0:T(1,128)S(1)} fusion(f32[4096]{0:T(1024)} %get-tuple-element.94, s32[]{:T(128)} %bitcast.121), kind=kLoop, calls=%fused_computation.2.clone.1 | loop fusion | bytes 516 | tf_op jit(solution)/shard_map/vmap()/gather
  35.4 1.4 %dynamic-slice_bitcast_fusion.2 = f32[1,64]{1,0:T(1,128)S(1)} fusion(f32[4096]{0:T(1024)} %get-tuple-element.94, s32[]{:T(128)} %bitcast.121), kind=kLoop, calls=%fused_computation.2.clone.1 | loop fusion | bytes 516 | tf_op jit(solution)/shard_map/vmap()/gather
  37.4 1.4 %dynamic-slice_bitcast_fusion.2 = f32[1,64]{1,0:T(1,128)S(1)} fusion(f32[4096]{0:T(1024)} %get-tuple-element.94, s32[]{:T(128)} %bitcast.121), kind=kLoop, calls=%fused_computation.2.clone.1 | loop fusion | bytes 516 | tf_op jit(solution)/shard_map/vmap()/gather
  39.4 1.4 %dynamic-slice_bitcast_fusion.2 = f32[1,64]{1,0:T(1,128)S(1)} fusion(f32[4096]{0:T(1024)} %get-tuple-element.94, s32[]{:T(128)} %bitcast.121), kind=kLoop, calls=%fused_computation.2.clone.1 | loop fusion | bytes 516 | tf_op jit(solution)/shard_map/vmap()/gather
  41.5 1.4 %dynamic-slice_bitcast_fusion.2 = f32[1,64]{1,0:T(1,128)S(1)} fusion(f32[4096]{0:T(1024)} %get-tuple-element.94, s32[]{:T(128)} %bitcast.121), kind=kLoop, calls=%fused_computation.2.clone.1 | loop fusion | bytes 516 | tf_op jit(solution)/shard_map/vmap()/gather
  43.5 1.4 %dynamic-slice_bitcast_fusion.2 = f32[1,64]{1,0:T(1,128)S(1)} fusion(f32[4096]{0:T(1024)} %get-tuple-element.94, s32[]{:T(128)} %bitcast.121), kind=kLoop, calls=%fused_computation.2.clone.1 | loop fusion | bytes 516 | tf_op jit(solution)/shard_map/vmap()/gather
  45.5 1.4 %dynamic-slice_bitcast_fusion.2 = f32[1,64]{1,0:T(1,128)S(1)} fusion(f32[4096]{0:T(1024)} %get-tuple-element.94, s32[]{:T(128)} %bitcast.121), kind=kLoop, calls=%fused_computation.2.clone.1 | loop fusion | bytes 516 | tf_op jit(solution)/shard_map/vmap()/gather
  47.6 1.4 %dynamic-slice_bitcast_fusion.2 = f32[1,64]{1,0:T(1,128)S(1)} fusion(f32[4096]{0:T(1024)} %get-tuple-element.94, s32[]{:T(128)} %bitcast.121), kind=kLoop, calls=%fused_computation.2.clone.1 | loop fusion | bytes 516 | tf_op jit(solution)/shard_map/vmap()/gather
  49.6 1.4 %dynamic-slice_bitcast_fusion.2 = f32[1,64]{1,0:T(1,128)S(1)} fusion(f32[4096]{0:T(1024)} %get-tuple-element.94, s32[]{:T(128)} %bitcast.121), kind=kLoop, calls=%fused_computation.2.clone.1 | loop fusion | bytes 516 | tf_op jit(solution)/shard_map/vmap()/gather
  51.7 1.4 %dynamic-slice_bitcast_fusion.2 = f32[1,64]{1,0:T(1,128)S(1)} fusion(f32[4096]{0:T(1024)} %get-tuple-element.94, s32[]{:T(128)} %bitcast.121), kind=kLoop, calls=%fused_computation.2.clone.1 | loop fusion | bytes 516 | tf_op jit(solution)/shard_map/vmap()/gather
  53.7 1.4 %dynamic-slice_bitcast_fusion.2 = f32[1,64]{1,0:T(1,128)S(1)} fusion(f32[4096]{0:T(1024)} %get-tuple-element.94, s32[]{:T(128)} %bitcast.121), kind=kLoop, calls=%fused_computation.2.clone.1 | loop fusion | bytes 516 | tf_op jit(solution)/shard_map/vmap()/gather
  55.7 1.4 %dynamic-slice_bitcast_fusion.2 = f32[1,64]{1,0:T(1,128)S(1)} fusion(f32[4096]{0:T(1024)} %get-tuple-element.94, s32[]{:T(128)} %bitcast.121), kind=kLoop, calls=%fused_computation.2.clone.1 | loop fusion | bytes 516 | tf_op jit(solution)/shard_map/vmap()/gather
  57.8 1.4 %dynamic-slice_bitcast_fusion.2 = f32[1,64]{1,0:T(1,128)S(1)} fusion(f32[4096]{0:T(1024)} %get-tuple-element.94, s32[]{:T(128)} %bitcast.121), kind=kLoop, calls=%fused_computation.2.clone.1 | loop fusion | bytes 516 | tf_op jit(solution)/shard_map/vmap()/gather
  59.8 1.4 %dynamic-slice_bitcast_fusion.2 = f32[1,64]{1,0:T(1,128)S(1)} fusion(f32[4096]{0:T(1024)} %get-tuple-element.94, s32[]{:T(128)} %bitcast.121), kind=kLoop, calls=%fused_computation.2.clone.1 | loop fusion | bytes 516 | tf_op jit(solution)/shard_map/vmap()/gather
  61.8 1.4 %dynamic-slice_bitcast_fusion.2 = f32[1,64]{1,0:T(1,128)S(1)} fusion(f32[4096]{0:T(1024)} %get-tuple-element.94, s32[]{:T(128)} %bitcast.121), kind=kLoop, calls=%fused_computation.2.clone.1 | loop fusion | bytes 516 | tf_op jit(solution)/shard_map/vmap()/gather
  63.9 1.4 %dynamic-slice_bitcast_fusion.2 = f32[1,64]{1,0:T(1,128)S(1)} fusion(f32[4096]{0:T(1024)} %get-tuple-element.94, s32[]{:T(128)} %bitcast.121), kind=kLoop, calls=%fused_computation.2.clone.1 | loop fusion | bytes 516 | tf_op jit(solution)/shard_map/vmap()/gather
  65.9 1.4 %dynamic-slice_bitcast_fusion.2 = f32[1,64]{1,0:T(1,128)S(1)} fusion(f32[4096]{0:T(1024)} %get-tuple-element.94, s32[]{:T(128)} %bitcast.121), kind=kLoop, calls=%fused_computation.2.clone.1 | loop fusion | bytes 516 | tf_op jit(solution)/shard_map/vmap()/gather
  68.0 1.4 %dynamic-slice_bitcast_fusion.2 = f32[1,64]{1,0:T(1,128)S(1)} fusion(f32[4096]{0:T(1024)} %get-tuple-element.94, s32[]{:T(128)} %bitcast.121), kind=kLoop, calls=%fused_computation.2.clone.1 | loop fusion | bytes 516 | tf_op jit(solution)/shard_map/vmap()/gather
  70.0 1.4 %dynamic-slice_bitcast_fusion.2 = f32[1,64]{1,0:T(1,128)S(1)} fusion(f32[4096]{0:T(1024)} %get-tuple-element.94, s32[]{:T(128)} %bitcast.121), kind=kLoop, calls=%fused_computation.2.clone.1 | loop fusion | bytes 516 | tf_op jit(solution)/shard_map/vmap()/gather
  72.0 1.4 %dynamic-slice_bitcast_fusion.2 = f32[1,64]{1,0:T(1,128)S(1)} fusion(f32[4096]{0:T(1024)} %get-tuple-element.94, s32[]{:T(128)} %bitcast.121), kind=kLoop, calls=%fused_computation.2.clone.1 | loop fusion | bytes 516 | tf_op jit(solution)/shard_map/vmap()/gather
  74.0 1.4 %dynamic-slice_bitcast_fusion.2 = f32[1,64]{1,0:T(1,128)S(1)} fusion(f32[4096]{0:T(1024)} %get-tuple-element.94, s32[]{:T(128)} %bitcast.121), kind=kLoop, calls=%fused_computation.2.clone.1 | loop fusion | bytes 516 | tf_op jit(solution)/shard_map/vmap()/gather
  76.1 1.4 %dynamic-slice_bitcast_fusion.2 = f32[1,64]{1,0:T(1,128)S(1)} fusion(f32[4096]{0:T(1024)} %get-tuple-element.94, s32[]{:T(128)} %bitcast.121), kind=kLoop, calls=%fused_computation.2.clone.1 | loop fusion | bytes 516 | tf_op jit(solution)/shard_map/vmap()/gather
  78.1 1.4 %dynamic-slice_bitcast_fusion.2 = f32[1,64]{1,0:T(1,128)S(1)} fusion(f32[4096]{0:T(1024)} %get-tuple-element.94, s32[]{:T(128)} %bitcast.121), kind=kLoop, calls=%fused_computation.2.clone.1 | loop fusion | bytes 516 | tf_op jit(solution)/shard_map/vmap()/gather
  80.2 1.4 %dynamic-slice_bitcast_fusion.2 = f32[1,64]{1,0:T(1,128)S(1)} fusion(f32[4096]{0:T(1024)} %get-tuple-element.94, s32[]{:T(128)} %bitcast.121), kind=kLoop, calls=%fused_computation.2.clone.1 | loop fusion | bytes 516 | tf_op jit(solution)/shard_map/vmap()/gather
  82.2 1.4 %dynamic-slice_bitcast_fusion.2 = f32[1,64]{1,0:T(1,128)S(1)} fusion(f32[4096]{0:T(1024)} %get-tuple-element.94, s32[]{:T(128)} %bitcast.121), kind=kLoop, calls=%fused_computation.2.clone.1 | loop fusion | bytes 516 | tf_op jit(solution)/shard_map/vmap()/gather
  84.9 3.5 %fusion.12 = (bf16[32,128,256]{2,1,0:T(8,128)(2,1)S(1)}, bf16[32,128,256]{2,1,0:T(8,128)(2,1)}, bf16[32,128,256]{2,1,0:T(8,128)(2,1)}) fusion(f32[32,256]{1,0:T(8,128)S(1)} %get-tuple-element.51, f32[128,256]{1,0:T(8,128)S(1)} %copy-done.5, f32[32,256]{1,0:T(8,128)S(1)} %get-tuple-element.50, f32[128,256]{1,0:T(8,128)S(1)} %copy-done.4), kind=kLoop, calls=%fused_computation.24 | loop fusion | flops 10485760 | bytes 6619136 | tf_op jit(solution)/shard_map/convert.13
  88.7 4.0 %select_multiply_fusion.1 = (f32[128,2048]{1,0:T(8,128)S(1)}, f32[128,2048]{1,0:T(8,128)S(1)}) fusion(f32[2048]{0:T(1024)S(1)} %broadcast_in_dim.27, s32[2048]{0:T(1024)S(1)} %add.265, s32[2048]{0:T(1024)S(1)} %add.264), kind=kLoop, calls=%fused_computation.30 | loop fusion | flops 2883584 | bytes 2121728 | tf_op jit(solution)/shard_map/mul | solution.py:84
  92.7 3.1 %subtract_convert_fusion.2 = (bf16[4,1,128,2048]{3,2,1,0:T(8,128)(2,1)}, bf16[4,1,128,2048]{3,2,1,0:T(8,128)(2,1)}) fusion(f32[4,2048]{1,0:T(4,128)S(1)} %get-tuple-element.41, f32[128,2048]{1,0:T(8,128)S(1)} %get-tuple-element.43, f32[4,2048]{1,0:T(4,128)S(1)} %get-tuple-element.40, f32[128,2048]{1,0:T(8,128)S(1)} %get-tuple-element.42), kind=kLoop, calls=%fused_computation.27 | loop fusion | flops 9437184 | bytes 6356992 | tf_op jit(solution)/shard_map/convert.14
  95.8 5.0 %gather_fusion.1 = bf16[4,32,64,256]{3,2,1,0:T(8,128)(2,1)} fusion(bf16[32,4,64,256]{3,2,1,0:T(8,128)(2,1)} %all-gather.2.cloned.1.call-done, s32[1024]{0:T(1024)S(1)} %pad_clamp_fusion), kind=kCustom, calls=%fused_computation.1 | custom fusion | bytes 8388624 | tf_op jit(solution)/shard_map/jit(_take)/gather | solution.py:110
  100.8 8.4 %convert_bitcast_fusion = bf16[4,32,64,512]{3,2,0,1:T(8,128)(2,1)} fusion(bf16[32,128,256]{2,1,0:T(8,128)(2,1)} %get-tuple-element.37, bf16[32,128,256]{2,1,0:T(8,128)(2,1)} %get-tuple-element.36, bf16[32,128,256]{2,1,0:T(8,128)(2,1)S(1)} %get-tuple-element.35, bf16[4,32,64,256]{3,2,1,0:T(8,128)(2,1)} %gather_fusion.1, ...), kind=kOutput, calls=%fused_computation.12 | convolution fusion | flops 2189426688 | bytes 18876420 | tf_op jit(solution)/shard_map/nsxk,nkv->snxv/dot_general | solution.py:121
  109.2 7.9 %copy.33 = bf16[4,32,64,512]{3,2,1,0:T(8,128)(2,1)} copy(bf16[4,32,64,512]{3,2,0,1:T(8,128)(2,1)} %convert_bitcast_fusion) | data formatting | bytes 16777216 | tf_op jit(solution)/shard_map/convert_element_type | solution.py:122
  117.1 5.9 %fusion.7 = f32[4,2,128,512]{3,2,1,0:T(8,128)S(1)} fusion(bf16[4,2048,512,1]{2,1,3,0:T(8,128)(2,1)} %bitcast.122, bf16[4,1,128,2048]{3,2,1,0:T(8,128)(2,1)S(1)} %copy-done.2, bf16[4,1,128,2048]{3,2,1,0:T(8,128)(2,1)S(1)} %copy-done.1), kind=kOutput, calls=%fused_computation.13 | convolution fusion | flops 2149580800 | bytes 14680064 | tf_op jit(solution)/shard_map/spkc,scv->spkv/dot_general | solution.py:123
  123.2 1.0 pad_maximum_fusion
  (108 shorter events, 23.2 us)
Async XLA Ops:
  6.5 77.3 %copy-start = (s32[4]{0:T(128)S(1)}, s32[4]{0:T(128)}, u32[]{:S(2)}) copy-start(s32[4]{0:T(128)} %param.16) | copy-start | bytes 52
  6.5 89.2 %all-gather.2.cloned.1.call-start = ((), (), s32[]{:S(2)}) async-start(), calls=%async_computation | async-start | bytes 4325376 | tf_op jit(solution)/shard_map/all_gather | solution.py:109
  13.2 2.6 %copy-start.8 = (bf16[2,128,4096,1,1]{2,1,0,4,3:T(8,128)(2,1)S(1)}, bf16[2,128,4096,1,1]{2,1,0,4,3:T(8,128)(2,1)}, u32[]{:S(2)}) copy-start(bf16[2,128,4096,1,1]{2,1,0,4,3:T(8,128)(2,1)} %constant.218) | copy-start | bytes 6291460
  15.8 2.1 %copy-start.6 = (s32[4,8,2]{1,2,0:T(2,128)S(1)}, s32[4,8,2]{1,2,0:T(2,128)}, u32[]{:S(2)}) copy-start(s32[4,8,2]{1,2,0:T(2,128)} %param.18) | copy-start | bytes 772
  15.8 67.9 %copy-start.7 = (s32[32]{0:T(128)S(1)}, s32[32]{0:T(128)}, u32[]{:S(2)}) copy-start(s32[32]{0:T(128)} %param.19) | copy-start | bytes 388
  15.8 69.0 %copy-start.4 = (f32[128,256]{1,0:T(8,128)S(1)}, f32[128,256]{1,0:T(8,128)}, u32[]{:S(2)}) copy-start(f32[128,256]{1,0:T(8,128)} %constant.214) | copy-start | bytes 393220
  15.8 69.0 %copy-start.5 = (f32[128,256]{1,0:T(8,128)S(1)}, f32[128,256]{1,0:T(8,128)}, u32[]{:S(2)}) copy-start(f32[128,256]{1,0:T(8,128)} %constant.215) | copy-start | bytes 393220
  109.2 7.9 %copy-start.1 = (bf16[4,1,128,2048]{3,2,1,0:T(8,128)(2,1)S(1)}, bf16[4,1,128,2048]{3,2,1,0:T(8,128)(2,1)}, u32[]{:S(2)}) copy-start(bf16[4,1,128,2048]{3,2,1,0:T(8,128)(2,1)} %get-tuple-element.29) | copy-start | bytes 6291460
  109.2 7.9 %copy-start.2 = (bf16[4,1,128,2048]{3,2,1,0:T(8,128)(2,1)S(1)}, bf16[4,1,128,2048]{3,2,1,0:T(8,128)(2,1)}, u32[]{:S(2)}) copy-start(bf16[4,1,128,2048]{3,2,1,0:T(8,128)(2,1)} %get-tuple-element.30) | copy-start | bytes 6291460
  117.1 5.9 %copy-start.3 = (f32[2,4,128,256]{3,2,1,0:T(8,128)S(1)}, f32[2,4,128,256]{3,2,1,0:T(8,128)}, u32[]{:S(2)}) copy-start(f32[2,4,128,256]{3,2,1,0:T(8,128)} %param.20) | copy-start | bytes 3145732
Sparse Core Ops, SparseCore 0:
  18.0 64.4 all-gather.1
where the time goes:
time: 133 us; the launch traced here: 131 us
  local copies, waits for them, and re-layouts  80.3 us (60%)
  other arithmetic  18.8 us (14%)
  between operations  16.2 us (12%)
  matrix products  15.6 us (12%)
    gather x96, local copies, waits for them, and re-layouts  65.1 us
    dot_general x1, matrix products, gather_part(): jnp.einsum('nsxk,nkv->snxv', picked, table, preferred_element_type=jnp.fl...  8.44 us
    convert_element_type x1, local copies, waits for them, and re-layouts, gather_part(): spread = spread.astype(jnp.bfloat16).reshape(slot_count, count * R, S)  7.87 us
    another operation x3, other arithmetic  7.63 us
    dot_general x1, matrix products, gather_part(): jnp.einsum('spkc,scv->spkv', row_part, spread, preferred_element_type=jnp...  5.89 us
    gather x1, local copies, waits for them, and re-layouts, shards(): picked = jnp.take(picked, slots // 2 % SG_C, axis=1)  4.99 us
    mul x1, other arithmetic, placed_rows(): base_cos = base_cos * scale  3.97 us
  transfers between devices with their start and end apart: 1, of which 0 were waited for; matrix products, arithmetic and copies ran while one was open for 59% of the time, Pallas kernels for 0%

commit v1 on v0

--- a/solution.py
+++ b/solution.py
@@ -5,6 +5,8 @@
 import ml_dtypes
 import numpy as np
 from jax import lax
+from jax.experimental import pallas as pl
+from jax.experimental.pallas import tpu as pltpu
 from jax.sharding import PartitionSpec as P
 
 N = 65536
@@ -71,9 +73,15 @@
     ).astype(jnp.bfloat16)
 
 
+def strip_windows(first_row, row_window):
+    picks = (first_row % F) // R
+    onehot = picks[:, None] == jnp.arange(F // R, dtype=jnp.int32)[None]
+    return jnp.sum(jnp.where(onehot[:, :, None], row_window.reshape(1, F // R, R), 0.0), 1)
+
+
 def placed_rows(first_row, row_start, rows, row_window, slot_rows):
     inner = jnp.arange(R, dtype=jnp.int32)
-    window = jax.vmap(lambda start: lax.dynamic_slice_in_dim(row_window, start, R))(first_row % F)
+    window = strip_windows(first_row, row_window)
     position = (first_row[:, None] + inner[None]).reshape(1, -1)
     shift = (row_start - first_row // (N // S)) & (S - 1)
     shift = jnp.where(shift < M, shift, shift - S)
@@ -88,6 +96,104 @@
     real = base_cos[None] * cos[:, None] - base_sin[None] * sin[:, None]
     imag = -(base_cos[None] * sin[:, None] + base_sin[None] * cos[:, None])
     return jnp.stack([real, imag], 1).astype(jnp.bfloat16)
+
+
+def flip(index, bits, size):
+    result = index
+    step = 1
+    while step < size:
+        if bits & step:
+            result = result + step - 2 * step * ((index // step) % 2)
+        step *= 2
+    return result
+
+
+def gather_kernel(chips, own_ref, out_ref, send_sem, recv_sem, own_sem):
+    row = lax.axis_index("frow")
+    col = lax.axis_index("fcol")
+    core = col % 2
+    chip = col // 2
+    sent = []
+
+    def device(row_bits, chip_bits, core_bits):
+        return (
+            flip(row, row_bits, 4),
+            2 * flip(chip, chip_bits, chips) + flip(core, core_bits, 2),
+        )
+
+    def place(row_bits, chip_bits, core_bits):
+        there = device(row_bits, chip_bits, core_bits)
+        return there[0] * (2 * chips) + there[1]
+
+    def send(item, target):
+        source = own_ref if item == (0, 0, 0) else out_ref.at[place(*item)]
+        copy = pltpu.make_async_remote_copy(
+            src_ref=source,
+            dst_ref=out_ref.at[place(*item)],
+            send_sem=send_sem.at[len(sent)],
+            recv_sem=recv_sem.at[place(*item)],
+            device_id=device(*target),
+            device_id_type=pl.DeviceIdType.MESH,
+        )
+        copy.start()
+        sent.append(copy)
+
+    def arrived(item):
+        there = out_ref.at[place(*item)]
+        pltpu.make_async_copy(there, there, recv_sem.at[place(*item)]).wait()
+
+    across, along, partner = (1, 0, 0), (2, 0, 0), (0, 0, 1)
+    peers = [across, along, partner] + [(0, bits, 0) for bits in range(1, chips)]
+    barrier = pltpu.get_barrier_semaphore()
+    for peer in peers:
+        pl.semaphore_signal(
+            barrier, inc=1, device_id=device(*peer), device_id_type=pl.DeviceIdType.MESH
+        )
+    pl.semaphore_wait(barrier, len(peers))
+    mine = (0, 0, 0)
+    for peer in peers[3:] + [across, along, partner]:
+        send(mine, peer)
+    keep = pltpu.make_async_copy(own_ref, out_ref.at[place(*mine)], own_sem)
+    keep.start()
+    for bits in range(chips):
+        if bits:
+            item = (0, bits, 0)
+            arrived(item)
+            for peer in (across, along, partner):
+                send(item, peer)
+        for first, other in ((1, along), (2, across)):
+            item = (first, bits, 0)
+            arrived(item)
+            if (bits % 2 == 0) == (first == 1):
+                send(item, other)
+            send(item, partner)
+    for bits in range(chips):
+        item = (3, bits, 0)
+        arrived(item)
+        send(item, partner)
+    for row_bits in range(4):
+        for bits in range(chips):
+            arrived((row_bits, bits, 1))
+    for copy in sent:
+        copy.wait_send()
+    keep.wait()
+
+
+def gather_all(own, sources, chips):
+    sends = sources - 1
+    return pl.pallas_call(
+        lambda *refs: gather_kernel(chips, *refs),
+        out_shape=jax.ShapeDtypeStruct((sources,) + own.shape, own.dtype),
+        in_specs=[pl.BlockSpec(memory_space=pltpu.VMEM)],
+        out_specs=pl.BlockSpec(memory_space=pl.ANY),
+        scratch_shapes=[
+            pltpu.SemaphoreType.DMA((sends,)),
+            pltpu.SemaphoreType.DMA((sources,)),
+            pltpu.SemaphoreType.DMA,
+        ],
+        compiler_params=pltpu.CompilerParams(collective_id=0, has_side_effects=True),
+        name="gather_all",
+    )(own)
 
 
 def shards(strips, row_window, col_window, sub_rows, sub_cols, facet_offsets, owner_map, screens):
@@ -106,7 +212,11 @@
         picked = picked.reshape(col_count, slot_count, R, 2 * M)
         picked = lax.all_gather(picked, "frow", tiled=True)
     else:
-        picked = lax.all_gather(own, ("frow", "fcol"))
+        if row_devices == 4 and col_count == 8:
+            picked = gather_all(own.reshape(SG_C * R, 2 * M), sources, col_count // 2)
+            picked = picked.reshape(sources, SG_C, R, 2 * M)
+        else:
+            picked = lax.all_gather(own, ("frow", "fcol"))
         picked = jnp.take(picked, slots // 2 % SG_C, axis=1)
     lanes = jnp.arange(2 * M, dtype=jnp.int32)
     signs = (1 - 2 * ((lanes[None] * (slots % 2)[:, None]) & 1)).astype(jnp.bfloat16)

time: 133 us -> 86.2 us (0.65); the launches traced: 131 us -> 85.8 us
  local copies, waits for them, and re-layouts: 80.3 us -> 15.2 us
  Pallas kernels: 0 us -> 38.4 us
  between operations: 16.2 us -> 2.83 us
  matrix products: 15.6 us -> 12 us
  other arithmetic: 18.8 us -> 17.4 us
    gather x96 -> x0, local copies, waits for them, and re-layouts: 65.1 us -> none
    pallas_call x0 -> x1, Pallas kernels: none -> 38.4 us  [gather_all(): pl.pallas_call(lambda *refs: gather_kernel(chips, *refs), out_shape=jax.S...]
    dot_general x1, matrix products: 5.89 us -> 2.32 us  [gather_part(): jnp.einsum('spkc,scv->spkv', row_part, spread, preferred_element_type=jnp...]
    another operation x3 -> x4, other arithmetic: 7.63 us -> 5.8 us
  transfers between devices with their start and end apart: 1 -> 0, of which waited for: 0 -> 0; matrix products, arithmetic and copies ran while one was open for 59% -> 0% of each run, Pallas kernels for 0% -> 0%
where the time goes in v1:
time: 86.2 us; the launch traced here: 85.8 us
  Pallas kernels  38.4 us (45%)
  other arithmetic  17.4 us (20%)
  local copies, waits for them, and re-layouts  15.2 us (18%)
  matrix products  12 us (14%)
  between operations  2.83 us (3%)
    pallas_call x1, Pallas kernels, gather_all(): pl.pallas_call(lambda *refs: gather_kernel(chips, *refs), out_shape=jax.S...  38.4 us
    dot_general x1, matrix products, gather_part(): jnp.einsum('nsxk,nkv->snxv', picked, table, preferred_element_type=jnp.fl...  8.42 us
    convert_element_type x1, local copies, waits for them, and re-layouts, gather_part(): spread = spread.astype(jnp.bfloat16).reshape(slot_count, count * R, S)  7.73 us
    another operation x4, other arithmetic  5.8 us
    gather x1, local copies, waits for them, and re-layouts, shards(): picked = jnp.take(picked, slots // 2 % SG_C, axis=1)  5.02 us
    mul x1, other arithmetic, placed_rows(): base_cos = base_cos * scale  3.97 us
    dot_general x1, matrix products, gather_part(): jnp.einsum('spkc,scv->spkv', row_part, spread, preferred_element_type=jnp...  2.32 us

profile of v1, /device:TPU:0, one launch (start us, length us, event | category | flops | bytes accessed | tf_op | source)
XLA Modules:
  0.0 85.8 jit_solution(5850393534561094906)
XLA Ops:
  0.0 0.0 copy-start
  0.0 1.3 %constant_dynamic-slice_fusion = s32[1,1,1]{1,2,0:T(1,128)} fusion(s32[4,8,2]{1,2,0:T(2,128)} %param.18, s32[]{:T(128)S(6)} %select_n.141, s32[]{:T(128)S(6)} %select_n.142), kind=kLoop, calls=%fused_computation.132 | loop fusion | bytes 16 | tf_op jit(solution)/shard_map/dynamic_slice | solution.py:207
  1.3 0.7 add_select_fusion
  1.9 0.7 neg.19
  2.7 1.3 %cosine_multiply_fusion = (f32[4,4096]{1,0:T(4,128)S(1)}, f32[4,4096]{1,0:T(4,128)S(1)}) fusion(s32[4096]{0:T(1024)S(1)} %get-tuple-element.38, s32[4]{0:T(128)} %param.17, s32[4096]{0:T(1024)S(1)} %get-tuple-element.39, f32[4096]{0:T(1024)} %param.15, f32[4096]{0:T(1024)S(1)} %neg.19), kind=kLoop, calls=%fused_computation.60 | loop fusion | flops 163840 | bytes 196624 | tf_op jit(solution)/shard_map/mul | solution.py:47
  4.0 0.0 copy-start.8
  4.0 1.5 %bitcast_convert_fusion.1 = (f32[64,4096]{1,0:T(8,128)S(1)}, f32[64,4096]{1,0:T(8,128)S(1)}) fusion(bf16[2,64,4096]{2,1,0:T(8,128)(2,1)} %param.13), kind=kLoop, calls=%fused_computation.45 | loop fusion | flops 524288 | bytes 3145728 | tf_op jit(solution)/shard_map/mul | solution.py:52
  5.5 1.0 %subtract_convert_fusion = (bf16[4,1,64,4096]{3,2,1,0:T(8,128)(2,1)S(1)}, bf16[4,1,64,4096]{3,2,1,0:T(8,128)(2,1)S(1)}) fusion(f32[4,4096]{1,0:T(4,128)S(1)} %get-tuple-element.25, f32[64,4096]{1,0:T(8,128)S(1)} %get-tuple-element.16, f32[4,4096]{1,0:T(4,128)S(1)} %get-tuple-element.24, f32[64,4096]{1,0:T(8,128)S(1)} %get-tuple-element.15), kind=kLoop, calls=%fused_computation.19 | loop fusion | flops 8388608 | bytes 6422528 | tf_op jit(solution)/shard_map/convert.4
  6.6 0.0 copy-done.8
  6.6 1.3 %fusion.13 = f32[4,2,64,2,128]{4,2,3,1,0:T(8,128)S(1)} fusion(bf16[2,128,4096,1,1]{2,1,0,4,3:T(8,128)(2,1)S(1)} %copy-done.8, bf16[4,1,64,4096]{3,2,1,0:T(8,128)(2,1)S(1)} %get-tuple-element.12, bf16[4,1,64,4096]{3,2,1,0:T(8,128)(2,1)S(1)} %get-tuple-element.11), kind=kOutput, calls=%fused_computation.26 | convolution fusion | flops 1082130432 | bytes 6815744 | tf_op jit(solution)/shard_map/dot_general | solution.py:54
  7.9 0.0 copy-start.7
  10.6 0.7 pad_maximum_fusion.1.refs_0_
  11.3 38.4 %gather_all.1 = bf16[32,256,256]{2,1,0:T(8,128)(2,1)} custom-call(bf16[256,256]{1,0:T(8,128)(2,1)} %pad_maximum_fusion.1.refs_0_), custom_call_target="tpu_custom_call" | custom-call | tf_op jit(solution)/shard_map/gather_all/pallas_call | solution.py:184
  49.7 0.0 copy-done.7
  49.7 0.1 and_select_fusion
  49.8 0.1 compare_and_fusion
  49.9 0.0 copy-start.6
  49.9 0.0 copy-start.3
  49.9 0.0 copy-start.4
  49.9 5.0 %gather_fusion.1 = bf16[4,32,64,256]{3,2,1,0:T(8,128)(2,1)} fusion(bf16[32,4,64,256]{3,2,1,0:T(8,128)(2,1)} %bitcast.102, s32[1024]{0:T(1024)S(1)} %pad_clamp_fusion), kind=kCustom, calls=%fused_computation.1 | custom fusion | bytes 8388624 | tf_op jit(solution)/shard_map/jit(_take)/gather | solution.py:220
  55.0 0.1 subtract_convert_fusion.3
  55.0 0.0 copy-done.6
  55.0 0.1 reshape.735
  55.1 0.2 fusion.27
  55.4 0.0 copy-done.3
  55.4 0.0 copy-done.4
  55.4 3.5 %fusion.12 = (bf16[32,128,256]{2,1,0:T(8,128)(2,1)S(1)}, bf16[32,128,256]{2,1,0:T(8,128)(2,1)}, bf16[32,128,256]{2,1,0:T(8,128)(2,1)}) fusion(f32[32,256]{1,0:T(8,128)S(1)} %get-tuple-element.37, f32[128,256]{1,0:T(8,128)S(1)} %copy-done.4, f32[32,256]{1,0:T(8,128)S(1)} %get-tuple-element.36, f32[128,256]{1,0:T(8,128)S(1)} %copy-done.3), kind=kLoop, calls=%fused_computation.22 | loop fusion | flops 10485760 | bytes 6619136 | tf_op jit(solution)/shard_map/convert.11
  58.9 8.4 %convert_bitcast_fusion = bf16[4,32,64,512]{3,2,0,1:T(8,128)(2,1)} fusion(bf16[32,128,256]{2,1,0:T(8,128)(2,1)} %get-tuple-element.21, bf16[32,128,256]{2,1,0:T(8,128)(2,1)} %get-tuple-element.20, bf16[32,128,256]{2,1,0:T(8,128)(2,1)S(1)} %get-tuple-element.19, bf16[4,32,64,256]{3,2,1,0:T(8,128)(2,1)} %gather_fusion.1, ...), kind=kOutput, calls=%fused_computation.10 | convolution fusion | flops 2189426688 | bytes 18876420 | tf_op jit(solution)/shard_map/nsxk,nkv->snxv/dot_general | solution.py:231
  67.3 7.7 %copy.26 = bf16[4,32,64,512]{3,2,1,0:T(8,128)(2,1)} copy(bf16[4,32,64,512]{3,2,0,1:T(8,128)(2,1)} %convert_bitcast_fusion) | data formatting | bytes 16777216 | tf_op jit(solution)/shard_map/convert_element_type | solution.py:232
  75.0 0.0 copy-done
  75.0 0.6 gather_fusion
  75.7 0.1 broadcast_in_dim.52
  75.8 0.1 add.249
  75.8 0.1 iota_add_fusion.2
  75.9 0.1 add.248
  76.0 0.3 fusion.32
  76.3 0.1 iota_compare_fusion
  76.4 0.0 copy-done.5
  76.4 0.1 broadcast_in_dim.54
  76.5 0.4 select_reduce_fusion
  76.9 0.1 broadcast_in_dim.57
  76.9 4.0 %select_multiply_fusion.1 = (f32[128,2048]{1,0:T(8,128)S(1)}, f32[128,2048]{1,0:T(8,128)S(1)}) fusion(f32[2048]{0:T(1024)S(1)} %broadcast_in_dim.57, s32[2048]{0:T(1024)S(1)} %add.249, s32[2048]{0:T(1024)S(1)} %add.248), kind=kLoop, calls=%fused_computation.28 | loop fusion | flops 2883584 | bytes 2121728 | tf_op jit(solution)/shard_map/mul | solution.py:92
  80.9 1.2 %subtract_convert_fusion.2 = (bf16[4,1,128,2048]{3,2,1,0:T(8,128)(2,1)S(1)}, bf16[4,1,128,2048]{3,2,1,0:T(8,128)(2,1)S(1)}) fusion(f32[4,2048]{1,0:T(4,128)S(1)} %get-tuple-element.27, f32[128,2048]{1,0:T(8,128)S(1)} %get-tuple-element.29, f32[4,2048]{1,0:T(4,128)S(1)} %get-tuple-element.26, f32[128,2048]{1,0:T(8,128)S(1)} %get-tuple-element.28), kind=kLoop, calls=%fused_computation.25 | loop fusion | flops 9437184 | bytes 6356992 | tf_op jit(solution)/shard_map/convert.12
  82.1 0.0 copy-done.1
  82.1 0.0 copy-start.2
  82.2 2.3 %fusion.7 = f32[4,2,128,512]{3,2,1,0:T(8,128)S(1)} fusion(bf16[4,2048,512,1]{2,1,3,0:T(8,128)(2,1)S(1)} %bitcast.103, bf16[4,1,128,2048]{3,2,1,0:T(8,128)(2,1)S(1)} %get-tuple-element.14, bf16[4,1,128,2048]{3,2,1,0:T(8,128)(2,1)S(1)} %get-tuple-element.13), kind=kOutput, calls=%fused_computation.11 | convolution fusion | flops 2149580800 | bytes 14680064 | tf_op jit(solution)/shard_map/spkc,scv->spkv/dot_general | solution.py:233
  84.5 0.2 multiply_subtract_fusion
  84.7 1.0 %pad_maximum_fusion = f32[2,4,128,256]{3,2,1,0:T(8,128)} fusion(f32[1,4,128,256]{3,2,1,0:T(8,128)S(1)} %get-tuple-element.10, f32[1,4,128,256]{3,2,1,0:T(8,128)S(1)} %get-tuple-element.9), kind=kLoop, calls=%fused_computation.29 | loop fusion | flops 262144 | bytes 2097152 | tf_op jit(solution)/shard_map/stack | solution.py:251
  (12 shorter events, 0.2 us)
Async XLA Ops:
  0.0 75.0 %copy-start = (s32[4]{0:T(128)S(1)}, s32[4]{0:T(128)}, u32[]{:S(2)}) copy-start(s32[4]{0:T(128)} %param.16) | copy-start | bytes 52
  4.0 2.6 %copy-start.8 = (bf16[2,128,4096,1,1]{2,1,0,4,3:T(8,128)(2,1)S(1)}, bf16[2,128,4096,1,1]{2,1,0,4,3:T(8,128)(2,1)}, u32[]{:S(2)}) copy-start(bf16[2,128,4096,1,1]{2,1,0,4,3:T(8,128)(2,1)} %constant.213) | copy-start | bytes 6291460
  7.9 41.8 %copy-start.7 = (s32[32]{0:T(128)S(1)}, s32[32]{0:T(128)}, u32[]{:S(2)}) copy-start(s32[32]{0:T(128)} %param.19) | copy-start | bytes 388
  49.9 5.1 %copy-start.6 = (s32[4,8,2]{1,2,0:T(2,128)S(1)}, s32[4,8,2]{1,2,0:T(2,128)}, u32[]{:S(2)}) copy-start(s32[4,8,2]{1,2,0:T(2,128)} %param.18) | copy-start | bytes 772
  49.9 5.4 %copy-start.3 = (f32[128,256]{1,0:T(8,128)S(1)}, f32[128,256]{1,0:T(8,128)}, u32[]{:S(2)}) copy-start(f32[128,256]{1,0:T(8,128)} %constant.209) | copy-start | bytes 393220
  49.9 5.4 %copy-start.4 = (f32[128,256]{1,0:T(8,128)S(1)}, f32[128,256]{1,0:T(8,128)}, u32[]{:S(2)}) copy-start(f32[128,256]{1,0:T(8,128)} %constant.210) | copy-start | bytes 393220
  67.3 9.1 %copy-start.5 = (f32[4096]{0:T(1024)S(1)}, f32[4096]{0:T(1024)}, u32[]{:S(2)}) copy-start(f32[4096]{0:T(1024)} %param.14) | copy-start | bytes 49156
  76.9 5.2 %copy-start.1 = (bf16[4,32,64,512]{3,2,1,0:T(8,128)(2,1)S(1)}, bf16[4,32,64,512]{3,2,1,0:T(8,128)(2,1)}, u32[]{:S(2)}) copy-start(bf16[4,32,64,512]{3,2,1,0:T(8,128)(2,1)} %copy.26) | copy-start | bytes 25165828
  82.1 2.3 %copy-start.2 = (f32[2,4,128,256]{3,2,1,0:T(8,128)S(1)}, f32[2,4,128,256]{3,2,1,0:T(8,128)}, u32[]{:S(2)}) copy-start(f32[2,4,128,256]{3,2,1,0:T(8,128)} %param.20) | copy-start | bytes 3145732
